TPU v7x, 32 devices: a whole 2x2x4 slice. The times are simulated.
32 devices in a mesh: mode: 4 (over y, x), rest: 8 (over z, core).
Axes of the slice: x: 2, y: 2, z: 4, core: 2. Of those that a mesh axis runs over, the one named last changes fastest.
Arguments:
- unfolded: float32 [512, 65536], P('mode', 'rest'), may hold values from -150 to 150
- start_block: float32 [512, 128], replicated, may hold values from -6 to 6
Outputs:
- triangle: float32 [512, 512], replicated
- factor: float32 [512, 128], replicated
- core: float32 [128, 65536], P('mode', 'rest')
All inputs are finite; a program needn't handle non-finite values.
Results may differ from a plain program's by a relative error of at most 0.0003.
Values sent between devices are 32-bit elements; how exact they have to be, the bound alone decides.
A program may use at most 64 MiB of HBM per device.

v0:
```python
import functools

import jax
import jax.numpy as jnp
from jax import lax
from jax.experimental import pallas as pl
from jax.experimental.pallas import tpu as pltpu
from jax.sharding import PartitionSpec as P

ITERS = 3
SUB = 8
STEP = 16
CHUNKS = 4
LANES = 128
F32 = jnp.float32
BF16 = jnp.bfloat16
MESH = pl.DeviceIdType.MESH


def parts3(x):
    hi = x.astype(BF16).astype(F32)
    rest = x - hi
    mid = rest.astype(BF16).astype(F32)
    return hi, mid, rest - mid


def nt(x, y):
    return lax.dot_general(x, y, (((1,), (1,)), ((), ())), preferred_element_type=F32)


def nn(x, y):
    return lax.dot_general(x, y, (((1,), (0,)), ((), ())), preferred_element_type=F32)


def dotf(x, y, dims):
    return lax.dot_general(
        x, y, (dims, ((), ())), precision=lax.Precision.HIGHEST, preferred_element_type=F32
    )


def eliminate(ref, row, col, width, block):
    r0 = pl.multiple_of(block * STEP, STEP)
    chunks = [ref[pl.ds(row + r0, STEP), pl.ds(col + c, LANES)] for c in range(0, width, LANES)]
    sub = lax.broadcasted_iota(jnp.int32, (STEP, LANES), 0)
    cols = [
        jnp.take_along_axis(chunks[0], jnp.full((STEP, LANES), r0 + k, jnp.int32), axis=1) for k in range(STEP)
    ]
    pivots = jnp.ones((STEP, LANES), F32)
    for k in range(STEP):
        p = cols[k][k : k + 1, :]
        f = jnp.where(sub > k, cols[k] * (1.0 / p), 0.0)
        pivots = jnp.where(sub == k, p, pivots)
        for j in range(k + 1, STEP):
            cols[j] = cols[j] - f * cols[j][k : k + 1, :]
        chunks = [v - f * v[k : k + 1, :] for v in chunks]
    s = lax.rsqrt(pivots)
    s = s * (1.5 - 0.5 * pivots * s * s)
    chunks = [v * s for v in chunks]
    v = jnp.concatenate(chunks, axis=1)
    ref[pl.ds(row + r0, STEP), pl.ds(col, width)] = v
    lane = lax.broadcasted_iota(jnp.int32, (STEP, LANES), 1)
    keep = lane >= r0 + STEP
    hi, mid, lo = parts3(v)
    lh, lm, ll = (jnp.where(keep, x[:, :LANES], 0.0) for x in (hi, mid, lo))
    left = jnp.concatenate([lh, lh, lm, lm, lh, ll], axis=0).astype(BF16)
    right = jnp.concatenate([hi, mid, hi, mid, lo, hi], axis=0).astype(BF16)
    upd = lax.dot_general(left, right, (((0,), (0,)), ((), ())), preferred_element_type=F32)
    ref[pl.ds(row, LANES), pl.ds(col, width)] -= upd


def block_pairs(count):
    return [(i, j) for i in range(count) for j in range(i, count)]


def solve_kernel(packed_ref, start_ref, work, factor_ref, basis_ref, gram_ref, aug):
    m, r = start_ref.shape
    rounds = m // LANES
    for at, (i, j) in enumerate(block_pairs(rounds)):
        piece = packed_ref[pl.ds(at * LANES, LANES), :]
        spot = (pl.ds(i * LANES, LANES), pl.ds(j * LANES, LANES))
        gram_ref[spot] = piece
        work[spot] = piece
        if i != j:
            gram_ref[spot[::-1]] = piece.T

    def refill(basis_t):
        image_t = dotf(basis_t, gram_ref[...], ((1,), (0,)))
        aug[:, pl.ds(0, r)] = dotf(image_t, image_t, ((1,), (1,)))
        aug[:, pl.ds(r, m)] = image_t

    refill(start_ref[...].T)
    for t in range(max(rounds - 1, ITERS)):
        base = t * LANES

        def step(block, carry):
            if t < rounds - 1:
                eliminate(work, base, base, m - base, block)
            if t < ITERS:
                eliminate(aug, 0, 0, r + m, block)
            return carry

        lax.fori_loop(0, LANES // STEP, step, 0)
        if t < rounds - 1:
            tail = m - base - LANES
            u = work[pl.ds(base, LANES), pl.ds(base + LANES, tail)]
            work[pl.ds(base + LANES, tail), pl.ds(base + LANES, tail)] -= dotf(u, u, ((0,), (0,)))
        if t < ITERS - 1:
            refill(aug[:, pl.ds(r, m)])
    basis_t = aug[:, pl.ds(r, m)]
    basis_ref[...] = basis_t
    factor_ref[...] = basis_t.T


def solve(packed, start_block):
    m, r = start_block.shape
    vmem = pl.BlockSpec(memory_space=pltpu.VMEM)
    return pl.pallas_call(
        solve_kernel,
        out_shape=(
            jax.ShapeDtypeStruct((m, m), F32),
            jax.ShapeDtypeStruct((m, r), F32),
            jax.ShapeDtypeStruct((r, m), F32),
        ),
        in_specs=[vmem, vmem],
        out_specs=(vmem, vmem, vmem),
        scratch_shapes=[pltpu.VMEM((m, m), F32), pltpu.VMEM((r, r + m), F32)],
        compiler_params=pltpu.CompilerParams(vmem_limit_bytes=32 * 1024 * 1024),
        cost_estimate=pl.CostEstimate(
            flops=12 * ITERS * r * m * (m + r) + 4 * m * m * m, bytes_accessed=8 * m * m, transcendentals=m
        ),
        name="solve",
    )(packed, start_block)


def gram_kernel(shape, total_cols, x_ref, full_out, out_ref, full, in_ref, got1, got2, got3, sum1, sum2,
                send, recv, row_send, row_recv, row_local, row_out):
    modes, cores, depth = shape
    me_mode = lax.axis_index("mode")
    me_rest = lax.axis_index("rest")
    me_core = lax.rem(me_rest, cores)
    me_z = me_rest // cores
    mine = (me_core, me_mode, me_z)
    sizes = (cores, modes, depth)
    rows = [in_ref.shape[0] // cores]
    rows.append(rows[0] // modes)
    rows.append(rows[1] // depth)

    def peer(stage, off):
        other = lax.rem(mine[stage] + off, sizes[stage])
        spot = [me_core, me_mode, me_z]
        spot[stage] = other
        return other, (spot[1], spot[2] * cores + spot[0])

    barrier = pltpu.get_barrier_semaphore()
    for stage in range(3):
        def greet(off, carry):
            _, device = peer(stage, off)
            pl.semaphore_signal(barrier, inc=1, device_id=device, device_id_type=MESH)
            return carry
        lax.fori_loop(1, sizes[stage], greet, 0)
    pl.semaphore_wait(barrier, sum(sizes) - 3)

    rows_dev = x_ref.shape[0]
    m, width = full.shape
    chunk = width // CHUNKS
    copies = []
    for c in range(CHUNKS):
        batch = []
        spot = (pl.ds(pl.multiple_of(me_mode * rows_dev, rows_dev), rows_dev), pl.ds(c * chunk, chunk))
        for off in range(1, modes):
            other, device = peer(1, off)
            batch.append(pltpu.make_async_remote_copy(
                src_ref=x_ref.at[:, pl.ds(pl.multiple_of(other * width + c * chunk, chunk), chunk)],
                dst_ref=full.at[spot],
                send_sem=row_send.at[c, off],
                recv_sem=row_recv.at[c, off],
                device_id=device,
                device_id_type=MESH,
            ))
        batch.append(pltpu.make_async_copy(
            x_ref.at[:, pl.ds(pl.multiple_of(me_mode * width + c * chunk, chunk), chunk)], full.at[spot], row_local.at[c]
        ))
        for copy in batch:
            copy.start()
        copies.append(batch)
    pairs = block_pairs(m // LANES)
    in_ref[...] = jnp.zeros_like(in_ref)
    stores = []
    for c in range(CHUNKS):
        for copy in copies[c]:
            copy.wait()
        part = (slice(None), pl.ds(c * chunk, chunk))
        store = pltpu.make_async_copy(full.at[part], full_out.at[part], row_out.at[c])
        store.start()
        stores.append(store)
        x = full[part]
        hi = x.astype(BF16)
        lo = (x - hi.astype(F32)).astype(BF16)
        for i in range(m // LANES):
            top = slice(i * LANES, (i + 1) * LANES)
            strip = nt(hi[top], hi[i * LANES :]) + (nt(hi[top], lo[i * LANES :]) + nt(lo[top], hi[i * LANES :]))
            for j in range(i, m // LANES):
                spot = pl.ds(pairs.index((i, j)) * LANES, LANES)
                in_ref[spot, :] += strip[:, (j - i) * LANES : (j - i + 1) * LANES]
    in_ref[...] = in_ref[...] / total_cols

    def at(start, size):
        return pl.ds(pl.multiple_of(start, SUB), size)

    def exchange(phase, stage, source, target):
        def copy(off):
            other, device = peer(stage, off)
            return pltpu.make_async_remote_copy(
                src_ref=source(other),
                dst_ref=target(mine[stage], off),
                send_sem=send.at[phase, off],
                recv_sem=recv.at[phase, off],
                device_id=device,
                device_id_type=MESH,
            )
        def begin(off, carry):
            copy(off).start()
            return carry
        def end(off, carry):
            copy(off).wait()
            return carry
        lax.fori_loop(1, sizes[stage], begin, 0)
        lax.fori_loop(1, sizes[stage], end, 0)

    def total(stage, source, got):
        def add(off, value):
            return value + got[off - 1]
        return lax.fori_loop(1, sizes[stage], add, source[at(mine[stage] * rows[stage], rows[stage]), :])

    exchange(0, 0, lambda o: in_ref.at[at(o * rows[0], rows[0])], lambda o, off: got1.at[off - 1])
    sum1[...] = total(0, in_ref, got1)
    exchange(1, 1, lambda o: sum1.at[at(o * rows[1], rows[1])], lambda o, off: got2.at[off - 1])
    sum2[...] = total(1, sum1, got2)
    exchange(2, 2, lambda o: sum2.at[at(o * rows[2], rows[2])], lambda o, off: got3.at[off - 1])
    start2 = me_core * rows[0] + me_mode * rows[1]
    start3 = start2 + me_z * rows[2]
    out_ref[at(start3, rows[2]), :] = total(2, sum2, got3)
    for phase, stage, start, size in ((3, 2, start3, rows[2]), (4, 1, start2, rows[1]), (5, 0, me_core * rows[0], rows[0])):
        block = out_ref.at[at(start, size)]
        exchange(phase, stage, lambda o: block, lambda o, off: block)


    for store in stores:
        store.wait()


def gram_sum(unfolded, modes, rest):
    rows_dev, cols_dev = unfolded.shape
    m, width = rows_dev * modes, cols_dev // modes
    cores = 2 if rest % 2 == 0 else 1
    depth = rest // cores
    count = len(block_pairs(m // LANES)) * LANES
    each = pl.cdiv(count, modes * rest * SUB) * SUB
    padded = each * modes * rest
    vmem = pl.BlockSpec(memory_space=pltpu.VMEM)
    anywhere = pl.BlockSpec(memory_space=pltpu.HBM)
    most = max(cores, modes, depth)
    return pl.pallas_call(
        functools.partial(gram_kernel, (modes, cores, depth), cols_dev * rest),
        out_shape=(jax.ShapeDtypeStruct((m, width), F32), jax.ShapeDtypeStruct((padded, LANES), F32)),
        in_specs=[anywhere],
        out_specs=(anywhere, vmem),
        scratch_shapes=[
            pltpu.VMEM((m, width), F32),
            pltpu.VMEM((padded, LANES), F32),
            pltpu.VMEM((max(cores - 1, 1), padded // cores, LANES), F32),
            pltpu.VMEM((max(modes - 1, 1), padded // (cores * modes), LANES), F32),
            pltpu.VMEM((max(depth - 1, 1), each, LANES), F32),
            pltpu.VMEM((padded // cores, LANES), F32),
            pltpu.VMEM((padded // (cores * modes), LANES), F32),
            pltpu.SemaphoreType.DMA((6, most)),
            pltpu.SemaphoreType.DMA((6, most)),
            pltpu.SemaphoreType.DMA((CHUNKS, modes)),
            pltpu.SemaphoreType.DMA((CHUNKS, modes)),
            pltpu.SemaphoreType.DMA((CHUNKS,)),
            pltpu.SemaphoreType.DMA((CHUNKS,)),
        ],
        compiler_params=pltpu.CompilerParams(
            collective_id=0, has_side_effects=True, vmem_limit_bytes=61 * 1024 * 1024
        ),
        name="gram_sum",
    )(unfolded)


def core_kernel(modes, basis_ref, full_ref, work_ref, tri_ref, core_ref, part, last, send, recv):
    me_mode = lax.axis_index("mode")
    me_rest = lax.axis_index("rest")
    rows_dev = core_ref.shape[0]
    width = full_ref.shape[1]
    chunk = width // CHUNKS
    others = [lax.rem(me_mode + off, modes) for off in range(1, modes)]
    barrier = pltpu.get_barrier_semaphore()
    for other in others:
        pl.semaphore_signal(barrier, inc=1, device_id=(other, me_rest), device_id_type=MESH)
    pl.semaphore_wait(barrier, modes - 1)
    basis = basis_ref[...]
    bh = basis.astype(BF16)
    bl = (basis - bh.astype(F32)).astype(BF16)
    copies = []
    for c in range(CHUNKS):
        cols = pl.ds(c * chunk, chunk)
        x = full_ref[:, cols]
        xh = x.astype(BF16)
        xl = (x - xh.astype(F32)).astype(BF16)
        part[:, cols] = nn(bh, xh) + (nn(bh, xl) + nn(bl, xh))
        mine = pl.ds(pl.multiple_of(me_mode * width + c * chunk, chunk), chunk)
        for at, other in enumerate(others):
            copy = pltpu.make_async_remote_copy(
                src_ref=part.at[pl.ds(pl.multiple_of(other * rows_dev, rows_dev), rows_dev), cols],
                dst_ref=core_ref.at[:, mine],
                send_sem=send.at[c, at],
                recv_sem=recv.at[c, at],
                device_id=(other, me_rest),
                device_id_type=MESH,
            )
            copy.start()
            copies.append(copy)
        core_ref[:, mine] = part[pl.ds(pl.multiple_of(me_mode * rows_dev, rows_dev), rows_dev), cols]
    rounds = work_ref.shape[0] // LANES
    base = (rounds - 1) * LANES
    last[...] = work_ref[pl.ds(base, LANES), pl.ds(base, LANES)]

    def step(block, carry):
        eliminate(last, 0, 0, LANES, block)
        return carry

    lax.fori_loop(0, LANES // STEP, step, 0)
    row = lax.broadcasted_iota(jnp.int32, (LANES, LANES), 0)
    col = lax.broadcasted_iota(jnp.int32, (LANES, LANES), 1)
    for i in range(rounds):
        for j in range(rounds):
            spot = (pl.ds(j * LANES, LANES), pl.ds(i * LANES, LANES))
            if j < i:
                tri_ref[spot] = jnp.zeros((LANES, LANES), F32)
                continue
            piece = last[...] if i == rounds - 1 else work_ref[spot[::-1]]
            tri_ref[spot] = (jnp.where(row <= col, piece, 0.0) if i == j else piece).T
    for copy in copies:
        copy.wait()


def core_exchange(basis_t, full_rows, work, modes):
    r = basis_t.shape[0]
    m, width = full_rows.shape
    vmem = pl.BlockSpec(memory_space=pltpu.VMEM)
    return pl.pallas_call(
        functools.partial(core_kernel, modes),
        out_shape=(jax.ShapeDtypeStruct((m, m), F32), jax.ShapeDtypeStruct((r // modes, width * modes), F32)),
        in_specs=[vmem, vmem, vmem],
        out_specs=(vmem, vmem),
        scratch_shapes=[
            pltpu.VMEM((r, width), F32),
            pltpu.VMEM((LANES, LANES), F32),
            pltpu.SemaphoreType.DMA((CHUNKS, modes)),
            pltpu.SemaphoreType.DMA((CHUNKS, modes)),
        ],
        compiler_params=pltpu.CompilerParams(
            collective_id=1, has_side_effects=True, vmem_limit_bytes=32 * 1024 * 1024
        ),
        name="core_exchange",
    )(basis_t, full_rows, work)


def per_device(unfolded, start_block):
    modes, rest = lax.axis_size("mode"), lax.axis_size("rest")
    full_rows, packed = gram_sum(unfolded, modes, rest)
    work, factor, basis_t = solve(packed, start_block)
    triangle, core = core_exchange(basis_t, full_rows, work, modes)
    return (triangle, factor, core)


def solution(mesh):
    return jax.shard_map(
        per_device,
        mesh=mesh,
        in_specs=(P("mode", "rest"), P()),
        out_specs=(P(), P(), P("mode", "rest")),
        check_vma=False,
    )
```

profile of v0, /device:TPU:0, one launch (start us, length us, event | category | flops | bytes accessed | tf_op | source)
XLA Modules:
  0.0 115.5 jit_solution(8261985962707418322)
XLA Ops:
  0.6 0.0 copy-start.2
  0.6 76.8 %gram_sum.1 = (f32[512,2048]{1,0:T(8,128)}, f32[1280,128]{1,0:T(8,128)}) custom-call(f32[128,8192]{1,0:T(8,128)} %x_ref.1), custom_call_target="tpu_custom_call" | custom-call | tf_op jit(solution)/shard_map/gram_sum/pallas_call | solution.py:263
  77.4 0.0 copy-start
  77.4 0.0 copy-done.2
  77.4 0.0 copy-start.1
  77.4 1.2 %copy-done.1 = f32[1280,128]{1,0:T(8,128)S(1)} copy-done((f32[1280,128]{1,0:T(8,128)S(1)}, f32[1280,128]{1,0:T(8,128)}, u32[]{:S(2)}) %copy-start.1) | copy-done | bytes 655384
  78.7 19.9 %solve.1 = (f32[512,512]{1,0:T(8,128)S(1)}, f32[512,128]{1,0:T(8,128)}, f32[128,512]{1,0:T(8,128)S(1)}) custom-call(f32[1280,128]{1,0:T(8,128)S(1)} %copy-done.1, f32[512,128]{1,0:T(8,128)S(1)} %copy-done.2), custom_call_target="tpu_custom_call" | custom-call | flops 2046820352 | bytes 2097152 | tf_op jit(solution)/shard_map/solve/pallas_call | solution.py:117
  98.5 0.0 copy-done
  98.5 15.0 %core_exchange.1 = (f32[512,512]{1,0:T(8,128)S(1)}, f32[32,8192]{1,0:T(8,128)S(1)}) custom-call(f32[128,512]{1,0:T(8,128)S(1)} %get-tuple-element.11.basis_ref, f32[512,2048]{1,0:T(8,128)S(1)} %copy-done, f32[512,512]{1,0:T(8,128)S(1)} %get-tuple-element.13.work_ref), custom_call_target="tpu_custom_call" | custom-call | tf_op jit(solution)/shard_map/core_exchange/pallas_call | solution.py:351
  113.5 1.0 copy.7
  114.5 1.0 copy.8
Async XLA Ops:
  0.6 76.8 %copy-start.2 = (f32[512,128]{1,0:T(8,128)S(1)}, f32[512,128]{1,0:T(8,128)}, u32[]{:S(2)}) copy-start(f32[512,128]{1,0:T(8,128)} %start_ref.1) | copy-start | bytes 786436
  77.4 21.1 %copy-start = (f32[512,2048]{1,0:T(8,128)S(1)}, f32[512,2048]{1,0:T(8,128)}, u32[]{:S(2)}) copy-start(f32[512,2048]{1,0:T(8,128)} %get-tuple-element.12.full_ref) | copy-start | bytes 12582916
  77.4 1.2 %copy-start.1 = (f32[1280,128]{1,0:T(8,128)S(1)}, f32[1280,128]{1,0:T(8,128)}, u32[]{:S(2)}) copy-start(f32[1280,128]{1,0:T(8,128)} %get-tuple-element.10.packed_ref) | copy-start | bytes 1966084
where the time goes:
time: 116 us; the launch traced here: 115 us
  Pallas kernels  112 us (97%)
  local copies, waits for them, and re-layouts  3.18 us (3%)
    pallas_call x1, Pallas kernels, gram_sum(): pl.pallas_call(functools.partial(gram_kernel, (modes, cores, depth), cols...  76.8 us
    pallas_call x1, Pallas kernels, solve(): pl.pallas_call(solve_kernel, out_shape=(jax.ShapeDtypeStruct((m, m), F32)...  19.9 us
    pallas_call x1, Pallas kernels, core_exchange(): pl.pallas_call(functools.partial(core_kernel, modes), out_shape=(jax.Shap...  15 us
    unnamed x8, local copies, waits for them, and re-layouts  3.18 us

commit v1 on v0

v1 whole, which is shorter than its diff:
```python
import functools

import jax
import jax.numpy as jnp
from jax import lax
from jax.experimental import pallas as pl
from jax.experimental.pallas import tpu as pltpu
from jax.sharding import PartitionSpec as P

ITERS = 3
SUB = 8
STEP = 16
SLICES = 2
LATE = 2
LANES = 128
F32 = jnp.float32
BF16 = jnp.bfloat16
MESH = pl.DeviceIdType.MESH


def parts3(x):
    hi = x.astype(BF16).astype(F32)
    rest = x - hi
    mid = rest.astype(BF16).astype(F32)
    return hi, mid, rest - mid


def nt(x, y):
    return lax.dot_general(x, y, (((1,), (1,)), ((), ())), preferred_element_type=F32)


def nn(x, y):
    return lax.dot_general(x, y, (((1,), (0,)), ((), ())), preferred_element_type=F32)


def dotf(x, y, dims):
    return lax.dot_general(
        x, y, (dims, ((), ())), precision=lax.Precision.HIGHEST, preferred_element_type=F32
    )


def eliminate(ref, row, col, width, block):
    r0 = pl.multiple_of(block * STEP, STEP)
    chunks = [ref[pl.ds(row + r0, STEP), pl.ds(col + c, LANES)] for c in range(0, width, LANES)]
    sub = lax.broadcasted_iota(jnp.int32, (STEP, LANES), 0)
    cols = [
        jnp.take_along_axis(chunks[0], jnp.full((STEP, LANES), r0 + k, jnp.int32), axis=1) for k in range(STEP)
    ]
    pivots = jnp.ones((STEP, LANES), F32)
    for k in range(STEP):
        p = cols[k][k : k + 1, :]
        f = jnp.where(sub > k, cols[k] * (1.0 / p), 0.0)
        pivots = jnp.where(sub == k, p, pivots)
        for j in range(k + 1, STEP):
            cols[j] = cols[j] - f * cols[j][k : k + 1, :]
        chunks = [v - f * v[k : k + 1, :] for v in chunks]
    s = lax.rsqrt(pivots)
    s = s * (1.5 - 0.5 * pivots * s * s)
    chunks = [v * s for v in chunks]
    v = jnp.concatenate(chunks, axis=1)
    ref[pl.ds(row + r0, STEP), pl.ds(col, width)] = v
    lane = lax.broadcasted_iota(jnp.int32, (STEP, LANES), 1)
    keep = lane >= r0 + STEP
    hi, mid, lo = parts3(v)
    lh, lm, ll = (jnp.where(keep, x[:, :LANES], 0.0) for x in (hi, mid, lo))
    left = jnp.concatenate([lh, lh, lm, lm, lh, ll], axis=0).astype(BF16)
    right = jnp.concatenate([hi, mid, hi, mid, lo, hi], axis=0).astype(BF16)
    upd = lax.dot_general(left, right, (((0,), (0,)), ((), ())), preferred_element_type=F32)
    ref[pl.ds(row, LANES), pl.ds(col, width)] -= upd


def block_pairs(count):
    return [(i, j) for i in range(count) for j in range(i, count)]


def cuts(width, weights):
    unit = width // sum(weights)
    starts = [unit * sum(weights[:k]) for k in range(len(weights))]
    return [(start, unit * weight) for start, weight in zip(starts, weights)]


def split(x):
    hi = x.astype(BF16)
    return hi, (x - hi.astype(F32)).astype(BF16)


def off_pairs(count):
    return [(i, j) for i in range(count) for j in range(i + 1, count)]


def owners_of(depth):
    return (depth // 4, depth // 2) if depth % 4 == 0 else (0, depth)


GATHER = (3, 2, 2, 1)
SCATTER = (1, 1, 2, 2, 2)


def kernel(shape, total_cols, x_ref, start_ref, tri_ref, factor_ref, core_ref,
           full, hi_ref, lo_ref, own, part, acc, tot, dacc, dtot, got_c, got_m, got_z, sum1, sum2, dgot_c, dgot_z,
           work, gram_ref, aug, begin,
           row_s, row_r, row_l, own_l, c_s, c_r, m_s, m_r, z_s, z_r, az_s, az_r, am_s, am_r, ac_s, ac_r,
           dc_s, dc_r, dz_s, dz_r, dm_s, dm_r, df_s, df_r, out_s, out_r):
    modes, cores, depth = shape
    me_mode = lax.axis_index("mode")
    me_rest = lax.axis_index("rest")
    me_core = lax.rem(me_rest, cores)
    me_z = me_rest // cores
    first_owner, owners = owners_of(depth)
    is_owner = jnp.logical_and(me_z >= first_owner, me_z < first_owner + owners)
    m, width = full.shape
    rows_dev, cols_dev = x_ref.shape
    rounds = m // LANES

    def mode_peer(off):
        other = lax.rem(me_mode + off, modes)
        return other, (other, me_rest)

    def core_peer(off):
        other = lax.rem(me_core + off, cores)
        return other, (me_mode, me_z * cores + other)

    def z_peer(off):
        other = lax.rem(me_z + off, depth)
        return other, (me_mode, other * cores + me_core)

    def remote(source, target, send, recv, device):
        return pltpu.make_async_remote_copy(
            src_ref=source, dst_ref=target, send_sem=send, recv_sem=recv, device_id=device, device_id_type=MESH
        )

    def at(start, size):
        return pl.ds(pl.multiple_of(start, SUB), size)

    def each_z(body):
        def step(off, carry):
            body(off)
            return carry
        lax.fori_loop(1, depth, step, 0)

    barrier = pltpu.get_barrier_semaphore()
    for peer, size in ((core_peer, cores), (mode_peer, modes)):
        for off in range(1, size):
            pl.semaphore_signal(barrier, inc=1, device_id=peer(off)[1], device_id_type=MESH)
    each_z(lambda off: pl.semaphore_signal(barrier, inc=1, device_id=z_peer(off)[1], device_id_type=MESH))
    pl.semaphore_wait(barrier, modes + cores + depth - 3)

    pieces = cuts(width, GATHER)
    mine_rows = pl.ds(pl.multiple_of(me_mode * rows_dev, rows_dev), rows_dev)
    arrivals = []
    for c, (start, size) in enumerate(pieces):
        spot = (mine_rows, pl.ds(start, size))
        batch = []
        for off in range(1, modes):
            other, device = mode_peer(off)
            batch.append(remote(
                x_ref.at[:, pl.ds(pl.multiple_of(other * width + start, LANES), size)], full.at[spot],
                row_s.at[c, off], row_r.at[c, off], device,
            ))
        batch.append(pltpu.make_async_copy(
            x_ref.at[:, pl.ds(pl.multiple_of(me_mode * width + start, LANES), size)], full.at[spot], row_l.at[c]
        ))
        for copy in batch:
            copy.start()
        arrivals.append(batch)
    loads = []
    for q in range(modes):
        cols = pl.ds(q * width, width)
        load = pltpu.make_async_copy(x_ref.at[:, cols], own.at[:, cols], own_l.at[q])
        load.start()
        loads.append(load)

    fetch = pltpu.make_async_copy(start_ref, begin, own_l.at[modes])
    fetch.start()
    dacc[...] = jnp.zeros_like(dacc)
    acc[...] = jnp.zeros_like(acc)
    for q in range(modes):
        loads[q].wait()
        h, l = split(own[:, pl.ds(q * width, width)])
        cross = nt(h, l)
        dacc[...] += nt(h, h) + (cross + cross.T)
    half = rows_dev // cores
    pending = []
    for off in range(1, cores):
        other, device = core_peer(off)
        copy = remote(dacc.at[at(other * half, half)], dgot_c.at[off - 1], dc_s.at[off], dc_r.at[off], device)
        copy.start()
        pending.append(copy)

    pairs = off_pairs(rounds)

    def absorb(c):
        for copy in arrivals[c]:
            copy.wait()
        start, size = pieces[c]
        cols = pl.ds(start, size)
        hi, lo = split(full[:, cols])
        hi_ref[:, cols] = hi
        lo_ref[:, cols] = lo
        for i in range(rounds - 1):
            top = slice(i * LANES, (i + 1) * LANES)
            rest = slice((i + 1) * LANES, m)
            strip = nt(hi[top], hi[rest]) + (nt(hi[top], lo[rest]) + nt(lo[top], hi[rest]))
            for j in range(i + 1, rounds):
                spot = pl.ds(pairs.index((i, j)) * LANES, LANES)
                acc[spot, :] += strip[:, (j - i - 1) * LANES : (j - i) * LANES]

    absorb(0)
    fetch.wait()
    for copy in pending:
        copy.wait()
    value = dacc[at(me_core * half, half), :]
    for off in range(1, cores):
        value = value + dgot_c[off - 1]
    dgot_z[me_z] = value

    def dz_copy(off):
        _, device = z_peer(off)
        return remote(dgot_z.at[me_z], dgot_z.at[me_z], dz_s.at[off], dz_r.at[off], device)

    each_z(lambda off: dz_copy(off).start())
    absorb(1)
    each_z(lambda off: dz_copy(off).wait())
    value = lax.fori_loop(1, depth, lambda z, v: v + dgot_z[z], dgot_z[0])
    dmine = at(me_mode * rows_dev + me_core * half, half)
    dtot[dmine, :] = value / total_cols
    for c in range(2, len(pieces)):
        absorb(c)

    padded = acc.shape[0]
    h0 = padded // SLICES
    h1 = h0 // cores
    h2 = h1 // modes
    h3 = h2 // owners
    sends = []

    stage_c = []
    for s in range(SLICES):
        batch = []
        for off in range(1, cores):
            other, device = core_peer(off)
            copy = remote(acc.at[at(s * h0 + other * h1, h1)], got_c.at[s, off - 1], c_s.at[s, off], c_r.at[s, off], device)
            copy.start()
            batch.append(copy)
        stage_c.append(batch)
    stage_m = []
    for s in range(SLICES):
        value = acc[at(s * h0 + me_core * h1, h1), :]
        for off, copy in enumerate(stage_c[s]):
            copy.wait_recv()
            value = value + got_c[s, off]
        sends += stage_c[s]
        sum1[s] = value
        batch = []
        for off in range(1, modes):
            other, device = mode_peer(off)
            copy = remote(sum1.at[s, at(other * h2, h2)], got_m.at[s, off - 1], m_s.at[s, off], m_r.at[s, off], device)
            copy.start()
            batch.append(copy)
        stage_m.append(batch)
    stage_d = []
    for off in range(1, modes):
        other, device = mode_peer(off)
        copy = remote(dtot.at[dmine], dtot.at[dmine], dm_s.at[off], dm_r.at[off], device)
        copy.start()
        stage_d.append(copy)

    def forward(ref, spot, send, recv):
        for off in range(1, cores):
            _, device = core_peer(off)
            copy = remote(ref.at[spot], ref.at[spot], send.at[off], recv.at[off], device)
            copy.start()
            sends.append(copy)
            relays.append(copy)

    relays = []
    forward(dtot, dmine, df_s.at[0], df_r.at[0])

    def z_copy(s, off):
        other, device = z_peer(off)
        return remote(
            sum2.at[s, at(jnp.clip(other - first_owner, 0, owners - 1) * h3, h3)], got_z.at[s, off],
            z_s.at[s, off], z_r.at[s, off], device,
        )

    def owned(z):
        return jnp.logical_and(z >= first_owner, z < first_owner + owners)

    def to_owner(off, act):
        pl.when(owned(z_peer(off)[0]))(act)

    for s in range(SLICES):
        value = sum1[s, at(me_mode * h2, h2), :]
        for off, copy in enumerate(stage_m[s]):
            copy.wait_recv()
            value = value + got_m[s, off]
        sends += stage_m[s]
        sum2[s] = value
        each_z(lambda off: to_owner(off, lambda: z_copy(s, off).start()))

    def my_start(s):
        return s * h0 + me_core * h1 + me_mode * h2

    def az_copy(s, off, z):
        _, device = z_peer(off)
        block = tot.at[at(my_start(s) + jnp.clip(z - first_owner, 0, owners - 1) * h3, h3)]
        return remote(block, block, az_s.at[s, off], az_r.at[s, off], device)

    for s in range(SLICES):
        @pl.when(is_owner)
        def _():
            each_z(lambda off: z_copy(s, off).wait_recv())
            spot = at(jnp.clip(me_z - first_owner, 0, owners - 1) * h3, h3)
            value = lax.fori_loop(1, depth, lambda off, v: v + got_z[s, off], sum2[s, spot, :])
            tot[at(my_start(s) + jnp.clip(me_z - first_owner, 0, owners - 1) * h3, h3), :] = value / total_cols
            each_z(lambda off: az_copy(s, off, me_z).start())

    for off, copy in enumerate(stage_d, 1):
        copy.wait_recv()
        source = lax.rem(me_mode - off + modes, modes)
        forward(dtot, at(source * rows_dev + me_core * half, half), df_s.at[off], df_r.at[off])
    sends += stage_d

    stage_a = []
    for s in range(SLICES):
        def arrive(off):
            source = lax.rem(me_z - off + depth, depth)
            pl.when(owned(source))(lambda: az_copy(s, off, source).wait_recv())
        each_z(arrive)
        block = at(my_start(s), h2)
        batch = []
        for off in range(1, modes):
            other, device = mode_peer(off)
            copy = remote(tot.at[block], tot.at[block], am_s.at[s, off], am_r.at[s, off], device)
            copy.start()
            batch.append(copy)
        forward(tot, block, ac_s.at[s, 0], ac_r.at[s, 0])
        stage_a.append(batch)
    for s in range(SLICES):
        for off, copy in enumerate(stage_a[s], 1):
            copy.wait_recv()
            source = lax.rem(me_mode - off + modes, modes)
            forward(tot, at(s * h0 + me_core * h1 + source * h2, h2), ac_s.at[s, off], ac_r.at[s, off])
        sends += stage_a[s]
    for copy in relays:
        copy.wait_recv()

    for i in range(rounds):
        spot = (pl.ds(i * LANES, LANES), pl.ds(i * LANES, LANES))
        piece = dtot[pl.ds(i * LANES, LANES), :]
        gram_ref[spot] = piece
        work[spot] = piece
    for where, (i, j) in enumerate(pairs):
        piece = tot[pl.ds(where * LANES, LANES), :]
        spot = (pl.ds(i * LANES, LANES), pl.ds(j * LANES, LANES))
        gram_ref[spot] = piece
        work[spot] = piece
        gram_ref[spot[::-1]] = piece.T

    r = start_ref.shape[1]

    def refill(basis_t):
        image_t = dotf(basis_t, gram_ref[...], ((1,), (0,)))
        aug[:, pl.ds(0, r)] = dotf(image_t, image_t, ((1,), (1,)))
        aug[:, pl.ds(r, m)] = image_t

    def schur(base):
        tail = m - base - LANES
        u = work[pl.ds(base, LANES), pl.ds(base + LANES, tail)]
        work[pl.ds(base + LANES, tail), pl.ds(base + LANES, tail)] -= dotf(u, u, ((0,), (0,)))

    early = max(rounds - LATE, 0)
    refill(begin[...].T)
    for t in range(max(early, ITERS)):
        base = t * LANES

        def step(block, carry):
            if t < early:
                eliminate(work, base, base, m - base, block)
            if t < ITERS:
                eliminate(aug, 0, 0, r + m, block)
            return carry

        lax.fori_loop(0, LANES // STEP, step, 0)
        if t < early:
            schur(base)
        if t < ITERS - 1:
            refill(aug[:, pl.ds(r, m)])
    basis_t = aug[:, pl.ds(r, m)]
    bh, bl = split(basis_t)
    out_rows = core_ref.shape[0]
    for c, (start, size) in enumerate(cuts(width, SCATTER)):
        cols = pl.ds(start, size)
        xh = hi_ref[:, cols]
        part[:, cols] = nn(bh, xh) + (nn(bh, lo_ref[:, cols]) + nn(bl, xh))
        mine = pl.ds(pl.multiple_of(me_mode * width + start, LANES), size)
        for off in range(1, modes):
            other, device = mode_peer(off)
            copy = remote(
                part.at[at(other * out_rows, out_rows), cols], core_ref.at[:, mine], out_s.at[c, off], out_r.at[c, off], device
            )
            copy.start()
            sends.append(copy)
            arrivals.append([copy])
        core_ref[:, mine] = part[at(me_mode * out_rows, out_rows), cols]
    factor_ref[...] = basis_t.T

    for t in range(early, rounds):
        base = t * LANES

        def late(block, carry):
            eliminate(work, base, base, m - base, block)
            return carry

        lax.fori_loop(0, LANES // STEP, late, 0)
        if t < rounds - 1:
            schur(base)
    row = lax.broadcasted_iota(jnp.int32, (LANES, LANES), 0)
    col = lax.broadcasted_iota(jnp.int32, (LANES, LANES), 1)
    for i in range(rounds):
        for j in range(rounds):
            spot = (pl.ds(j * LANES, LANES), pl.ds(i * LANES, LANES))
            if j < i:
                tri_ref[spot] = jnp.zeros((LANES, LANES), F32)
                continue
            piece = work[spot[::-1]]
            tri_ref[spot] = (jnp.where(row <= col, piece, 0.0) if i == j else piece).T

    for copy in sends:
        copy.wait_send()
    for s in range(SLICES):
        each_z(lambda off: to_owner(off, lambda: z_copy(s, off).wait_send()))

        @pl.when(is_owner)
        def _():
            each_z(lambda off: az_copy(s, off, me_z).wait_send())
    for batch in arrivals[len(pieces):]:
        for copy in batch:
            copy.wait_recv()


def program(unfolded, start_block, modes, rest):
    rows_dev, cols_dev = unfolded.shape
    m, r = start_block.shape
    width = cols_dev // modes
    cores = 2 if rest % 2 == 0 else 1
    depth = rest // cores
    owners = owners_of(depth)[1]
    unit = SLICES * cores * modes * owners * SUB
    padded = pl.cdiv(len(off_pairs(m // LANES)) * LANES, unit) * unit
    h1 = padded // SLICES // cores
    h2 = h1 // modes
    h3 = h2 // owners
    half = rows_dev // cores
    vmem = pl.BlockSpec(memory_space=pltpu.VMEM)
    dma = pltpu.SemaphoreType.DMA
    few = max(cores - 1, 1)
    two = lambda *shape: [dma(shape), dma(shape)]
    return pl.pallas_call(
        functools.partial(kernel, (modes, cores, depth), cols_dev * rest),
        out_shape=(
            jax.ShapeDtypeStruct((m, m), F32),
            jax.ShapeDtypeStruct((m, r), F32),
            jax.ShapeDtypeStruct((r // modes, cols_dev), F32),
        ),
        in_specs=[pl.BlockSpec(memory_space=pltpu.HBM)] * 2,
        out_specs=(vmem, vmem, vmem),
        scratch_shapes=[
            pltpu.VMEM((m, width), F32),
            pltpu.VMEM((m, width), BF16),
            pltpu.VMEM((m, width), BF16),
            pltpu.VMEM((rows_dev, cols_dev), F32),
            pltpu.VMEM((r, width), F32),
            pltpu.VMEM((padded, LANES), F32),
            pltpu.VMEM((padded, LANES), F32),
            pltpu.VMEM((rows_dev, rows_dev), F32),
            pltpu.VMEM((m, LANES), F32),
            pltpu.VMEM((SLICES, few, h1, LANES), F32),
            pltpu.VMEM((SLICES, modes, h2, LANES), F32),
            pltpu.VMEM((SLICES, depth, h3, LANES), F32),
            pltpu.VMEM((SLICES, h1, LANES), F32),
            pltpu.VMEM((SLICES, h2, LANES), F32),
            pltpu.VMEM((few, half, LANES), F32),
            pltpu.VMEM((depth, half, LANES), F32),
            pltpu.VMEM((m, m), F32),
            pltpu.VMEM((m, m), F32),
            pltpu.VMEM((r, r + m), F32),
            pltpu.VMEM((m, r), F32),
            *two(len(GATHER), modes), dma((len(GATHER),)), dma((modes + 1,)),
            *two(SLICES, cores), *two(SLICES, modes), *two(SLICES, depth), *two(SLICES, depth),
            *two(SLICES, modes), *two(SLICES, modes, cores),
            *two(cores), *two(depth), *two(modes), *two(modes, cores),
            *two(len(SCATTER), modes),
        ],
        compiler_params=pltpu.CompilerParams(
            collective_id=0, has_side_effects=True, vmem_limit_bytes=48 * 1024 * 1024
        ),
        name="truncate",
    )(unfolded, start_block)


def per_device(unfolded, start_block):
    return program(unfolded, start_block, lax.axis_size("mode"), lax.axis_size("rest"))


def solution(mesh):
    return jax.shard_map(
        per_device,
        mesh=mesh,
        in_specs=(P("mode", "rest"), P()),
        out_specs=(P(), P(), P("mode", "rest")),
        check_vma=False,
    )
```

time: 116 us -> 106 us (0.914)
  Pallas kernels: 112 us -> 101 us
    pallas_call x3 -> x1, Pallas kernels: 112 us -> 101 us  [program(): pl.pallas_call(functools.partial(kernel, (modes, cores, depth), cols_dev...]
    unnamed x8 -> x5, local copies, waits for them, and re-layouts: 3.18 us -> 3.59 us
where the time goes in v1:
time: 106 us
  Pallas kernels  101 us (95%)
  local copies, waits for them, and re-layouts  3.59 us (3%)
    pallas_call x1, Pallas kernels, program(): pl.pallas_call(functools.partial(kernel, (modes, cores, depth), cols_dev...  101 us
    unnamed x5, local copies, waits for them, and re-layouts  3.59 us

profile of v1, /device:TPU:0, one launch (start us, length us, event | category | flops | bytes accessed | tf_op | source)
XLA Modules:
  0.0 105.6 jit_solution(8448797049561570753)
XLA Ops:
  0.6 0.0 copy-start
  0.6 0.9 copy-done
  1.6 101.3 %truncate.1 = (f32[512,512]{1,0:T(8,128)S(1)}, f32[512,128]{1,0:T(8,128)S(1)}, f32[32,8192]{1,0:T(8,128)S(1)}) custom-call(f32[128,8192]{1,0:T(8,128)} %x_ref.1, f32[512,128]{1,0:T(8,128)S(1)} %copy-done), custom_call_target="tpu_custom_call" | custom-call | tf_op jit(solution)/shard_map/truncate/pallas_call | solution.py:459
  102.9 1.0 copy.8
  103.9 0.7 copy.9
  104.6 1.0 copy.10
Async XLA Ops:
  0.6 1.0 copy-start

commit v2 on v1

--- a/solution.py
+++ b/solution.py
@@ -9,9 +9,9 @@
 
 ITERS = 3
 SUB = 8
-STEP = 16
+MACRO = 32
+MICRO = 16
 SLICES = 2
-LATE = 2
 LANES = 128
 F32 = jnp.float32
 BF16 = jnp.bfloat16
@@ -39,38 +39,97 @@
     )
 
 
-def eliminate(ref, row, col, width, block):
-    r0 = pl.multiple_of(block * STEP, STEP)
-    chunks = [ref[pl.ds(row + r0, STEP), pl.ds(col + c, LANES)] for c in range(0, width, LANES)]
-    sub = lax.broadcasted_iota(jnp.int32, (STEP, LANES), 0)
-    cols = [
-        jnp.take_along_axis(chunks[0], jnp.full((STEP, LANES), r0 + k, jnp.int32), axis=1) for k in range(STEP)
-    ]
-    pivots = jnp.ones((STEP, LANES), F32)
-    for k in range(STEP):
-        p = cols[k][k : k + 1, :]
-        f = jnp.where(sub > k, cols[k] * (1.0 / p), 0.0)
-        pivots = jnp.where(sub == k, p, pivots)
-        for j in range(k + 1, STEP):
-            cols[j] = cols[j] - f * cols[j][k : k + 1, :]
-        chunks = [v - f * v[k : k + 1, :] for v in chunks]
-    s = lax.rsqrt(pivots)
-    s = s * (1.5 - 0.5 * pivots * s * s)
-    chunks = [v * s for v in chunks]
-    v = jnp.concatenate(chunks, axis=1)
-    ref[pl.ds(row + r0, STEP), pl.ds(col, width)] = v
-    lane = lax.broadcasted_iota(jnp.int32, (STEP, LANES), 1)
-    keep = lane >= r0 + STEP
-    hi, mid, lo = parts3(v)
-    lh, lm, ll = (jnp.where(keep, x[:, :LANES], 0.0) for x in (hi, mid, lo))
+def spread(x, row):
+    return jnp.broadcast_to(x[row : row + 1, :], x.shape)
+
+
+def column(x, lane):
+    return jnp.broadcast_to(x[:, lane : lane + 1], x.shape)
+
+
+def invert_block(ref, base, r0):
+    tiles = MACRO // SUB
+    rows = [ref[pl.ds(base + r0 + SUB * h, SUB), :] for h in range(tiles)]
+    lane = lax.broadcasted_iota(jnp.int32, (SUB, LANES), 1)
+    sub = lax.broadcasted_iota(jnp.int32, (SUB, LANES), 0)
+    pivots = [None] * tiles
+
+    def retire(k, f):
+        t, s = divmod(k, SUB)
+        here = lane == r0 + k
+        row = jnp.where(here, 1.0, spread(rows[t], s))
+        for h in range(t, tiles):
+            if h == t:
+                old = jnp.where(here & (sub >= s), jnp.where(sub == s, 1.0, 0.0), rows[h])
+            else:
+                old = jnp.where(here, 0.0, rows[h])
+            rows[h] = old - f[h] * row
+
+    for first in range(0, MACRO, MICRO):
+        stop = first + MICRO
+        cols = {(j, h): column(rows[h], r0 + j) for j in range(first, stop) for h in range(j // SUB, tiles)}
+        unit = spread(cols[first, first // SUB], first % SUB)
+        scale = 1.0 / unit
+        cols = {spot: x * scale for spot, x in cols.items()}
+        for k in range(first, stop, 2):
+            t, s = divmod(k, SUB)
+            p = spread(cols[k, t], s)
+            a = spread(cols[k, t], s + 1)
+            b = spread(cols[k + 1, t], s + 1)
+            det = p * b - a * a
+            inv_p = 1.0 / p
+            inv_q = p * (1.0 / det)
+            found = jnp.where(sub == s, p, det * inv_p) * unit
+            pivots[t] = found if s == 0 else jnp.where(sub >= s, found, pivots[t])
+            f = {h: cols[k, h] * inv_p for h in range(t, tiles)}
+            f[t] = jnp.where(sub > s, f[t], 0.0)
+            second = {h: cols[k + 1, h] - f[h] * a for h in range(t, tiles)}
+            g = {h: second[h] * inv_q for h in range(t, tiles)}
+            g[t] = jnp.where(sub > s + 1, g[t], 0.0)
+            for j in range(k + 2, stop):
+                one = spread(cols[k, j // SUB], j % SUB)
+                two = spread(second[j // SUB], j % SUB)
+                for h in range(j // SUB, tiles):
+                    cols[j, h] = (cols[j, h] - f[h] * one) - g[h] * two
+            retire(k, f)
+            retire(k + 1, g)
+    for h in range(tiles):
+        s = lax.rsqrt(pivots[h])
+        s = s * (1.5 - 0.5 * pivots[h] * s * s)
+        rows[h] = rows[h] * s
+        ref[pl.ds(base + r0 + SUB * h, SUB), :] = rows[h]
+    size = LANES - r0 - MACRO
+    if size == 0:
+        return
+    lane = lax.broadcasted_iota(jnp.int32, (MACRO, LANES), 1)
+    row = lax.broadcasted_iota(jnp.int32, (MACRO, LANES), 0)
+    keep = lane >= r0 + MACRO
+    lower = keep | (lane <= row + r0)
+    pieces = parts3(jnp.concatenate(rows, axis=0))
+    lh, lm, ll = (jnp.where(keep, x, 0.0) for x in pieces)
+    rh, rm, rl = (jnp.where(lower, x, 0.0) for x in pieces)
     left = jnp.concatenate([lh, lh, lm, lm, lh, ll], axis=0).astype(BF16)
-    right = jnp.concatenate([hi, mid, hi, mid, lo, hi], axis=0).astype(BF16)
+    right = jnp.concatenate([rh, rm, rh, rm, rl, rh], axis=0).astype(BF16)
     upd = lax.dot_general(left, right, (((0,), (0,)), ((), ())), preferred_element_type=F32)
-    ref[pl.ds(row, LANES), pl.ds(col, width)] -= upd
-
-
-def block_pairs(count):
-    return [(i, j) for i in range(count) for j in range(i, count)]
+    lane = lax.broadcasted_iota(jnp.int32, (size, LANES), 1)
+    inside = (lane >= r0) & (lane < r0 + MACRO)
+    spot = pl.ds(base + r0 + MACRO, size)
+    ref[spot, :] = jnp.where(inside, 0.0, ref[spot, :]) - upd[r0 + MACRO :, :]
+
+
+def invert(ref, base):
+    for r0 in range(0, LANES, MACRO):
+        invert_block(ref, base, r0)
+
+
+def stack(pieces, axis=0):
+    return jnp.concatenate(pieces, axis=axis).astype(BF16)
+
+
+def lower_part(x):
+    row = lax.broadcasted_iota(jnp.int32, x.shape, 0)
+    col = lax.broadcasted_iota(jnp.int32, x.shape, 1)
+    return jnp.where(row >= col, x, 0.0)
 
 
 def cuts(width, weights):
@@ -98,7 +157,7 @@
 
 def kernel(shape, total_cols, x_ref, start_ref, tri_ref, factor_ref, core_ref,
            full, hi_ref, lo_ref, own, part, acc, tot, dacc, dtot, got_c, got_m, got_z, sum1, sum2, dgot_c, dgot_z,
-           work, gram_ref, aug, begin,
+           work, gram_h, gram_m, gram_l, small, panel, basis, begin,
            row_s, row_r, row_l, own_l, c_s, c_r, m_s, m_r, z_s, z_r, az_s, az_r, am_s, am_r, ac_s, ac_r,
            dc_s, dc_r, dz_s, dz_r, dm_s, dm_r, df_s, df_r, out_s, out_r):
     modes, cores, depth = shape
@@ -274,6 +333,11 @@
             relays.append(copy)
 
     relays = []
+
+    def keep_gram(spot, piece):
+        for ref, value in zip((gram_h, gram_m, gram_l), parts3(piece)):
+            ref[spot] = value.astype(BF16)
+
     forward(dtot, dmine, df_s.at[0], df_r.at[0])
 
     def z_copy(s, off):
@@ -320,6 +384,16 @@
         source = lax.rem(me_mode - off + modes, modes)
         forward(dtot, at(source * rows_dev + me_core * half, half), df_s.at[off], df_r.at[off])
     sends += stage_d
+    for copy in relays:
+        copy.wait_recv()
+    relays.clear()
+    for i in range(rounds):
+        spot = (pl.ds(i * LANES, LANES), pl.ds(i * LANES, LANES))
+        piece = dtot[pl.ds(i * LANES, LANES), :]
+        keep_gram(spot, piece)
+        work[spot] = piece
+    panel[pl.ds(0, LANES), :] = dtot[pl.ds(0, LANES), :]
+    invert(panel, 0)
 
     stage_a = []
     for s in range(SLICES):
@@ -345,48 +419,35 @@
     for copy in relays:
         copy.wait_recv()
 
-    for i in range(rounds):
-        spot = (pl.ds(i * LANES, LANES), pl.ds(i * LANES, LANES))
-        piece = dtot[pl.ds(i * LANES, LANES), :]
-        gram_ref[spot] = piece
-        work[spot] = piece
     for where, (i, j) in enumerate(pairs):
         piece = tot[pl.ds(where * LANES, LANES), :]
         spot = (pl.ds(i * LANES, LANES), pl.ds(j * LANES, LANES))
-        gram_ref[spot] = piece
         work[spot] = piece
-        gram_ref[spot[::-1]] = piece.T
-
-    r = start_ref.shape[1]
-
-    def refill(basis_t):
-        image_t = dotf(basis_t, gram_ref[...], ((1,), (0,)))
-        aug[:, pl.ds(0, r)] = dotf(image_t, image_t, ((1,), (1,)))
-        aug[:, pl.ds(r, m)] = image_t
-
-    def schur(base):
-        tail = m - base - LANES
-        u = work[pl.ds(base, LANES), pl.ds(base + LANES, tail)]
-        work[pl.ds(base + LANES, tail), pl.ds(base + LANES, tail)] -= dotf(u, u, ((0,), (0,)))
-
-    early = max(rounds - LATE, 0)
-    refill(begin[...].T)
-    for t in range(max(early, ITERS)):
-        base = t * LANES
-
-        def step(block, carry):
-            if t < early:
-                eliminate(work, base, base, m - base, block)
-            if t < ITERS:
-                eliminate(aug, 0, 0, r + m, block)
-            return carry
-
-        lax.fori_loop(0, LANES // STEP, step, 0)
-        if t < early:
-            schur(base)
-        if t < ITERS - 1:
-            refill(aug[:, pl.ds(r, m)])
-    basis_t = aug[:, pl.ds(r, m)]
+        keep_gram(spot, piece)
+        keep_gram(spot[::-1], piece.T)
+
+    basis[...] = begin[...].T
+    r = basis.shape[0]
+
+    def iterate(t, carry):
+        old = stack(parts3(basis[...]))
+        one = nn(old, gram_h[...])
+        two = nn(old[: 2 * r], gram_m[...])
+        image = one[:r] + ((one[r : 2 * r] + two[:r]) + (one[2 * r :] + (two[r:] + nn(old[:r], gram_l[...]))))
+        ih, im, il = parts3(image)
+        new = stack([ih, im, il])
+        q = nt(new, new[: 2 * r])
+        low = q[2 * r :, :r]
+        small[...] = q[:r, :r] + ((q[:r, r:] + q[r : 2 * r, :r]) + (q[r : 2 * r, r:] + (low + low.T)))
+        invert(small, 0)
+        wh, wm, wl = parts3(lower_part(small[...]))
+        high = nn(stack([stack([wh, wh], 1), stack([wm, wm], 1)]), new[: 2 * r])
+        rest = nn(stack([wl, wh], 1), stack([ih, il]))
+        basis[...] = high[:r] + (high[r:] + rest)
+        return carry
+
+    lax.fori_loop(0, ITERS, iterate, 0)
+    basis_t = basis[...]
     bh, bl = split(basis_t)
     out_rows = core_ref.shape[0]
     for c, (start, size) in enumerate(cuts(width, SCATTER)):
@@ -405,16 +466,17 @@
         core_ref[:, mine] = part[at(me_mode * out_rows, out_rows), cols]
     factor_ref[...] = basis_t.T
 
-    for t in range(early, rounds):
+    for t in range(rounds):
         base = t * LANES
-
-        def late(block, carry):
-            eliminate(work, base, base, m - base, block)
-            return carry
-
-        lax.fori_loop(0, LANES // STEP, late, 0)
+        here = pl.ds(base, LANES)
+        if t > 0:
+            panel[here, :] = work[here, here]
+            invert(panel, base)
         if t < rounds - 1:
-            schur(base)
+            tail = pl.ds(base + LANES, m - base - LANES)
+            u = dotf(lower_part(panel[here, :]), work[here, tail], ((1,), (0,)))
+            work[here, tail] = u
+            work[tail, tail] -= dotf(u, u, ((0,), (0,)))
     row = lax.broadcasted_iota(jnp.int32, (LANES, LANES), 0)
     col = lax.broadcasted_iota(jnp.int32, (LANES, LANES), 1)
     for i in range(rounds):
@@ -422,9 +484,11 @@
             spot = (pl.ds(j * LANES, LANES), pl.ds(i * LANES, LANES))
             if j < i:
                 tri_ref[spot] = jnp.zeros((LANES, LANES), F32)
-                continue
-            piece = work[spot[::-1]]
-            tri_ref[spot] = (jnp.where(row <= col, piece, 0.0) if i == j else piece).T
+            elif j > i:
+                tri_ref[spot] = work[spot[::-1]].T
+            else:
+                piece = panel[pl.ds(i * LANES, LANES), :]
+                tri_ref[spot] = jnp.where(row < col, piece, jnp.where(row == col, 1.0 / piece, 0.0)).T
 
     for copy in sends:
         copy.wait_send()
@@ -483,8 +547,10 @@
             pltpu.VMEM((few, half, LANES), F32),
             pltpu.VMEM((depth, half, LANES), F32),
             pltpu.VMEM((m, m), F32),
-            pltpu.VMEM((m, m), F32),
-            pltpu.VMEM((r, r + m), F32),
+            *[pltpu.VMEM((m, m), BF16)] * 3,
+            pltpu.VMEM((r, r), F32),
+            pltpu.VMEM((m, LANES), F32),
+            pltpu.VMEM((r, m), F32),
             pltpu.VMEM((m, r), F32),
             *two(len(GATHER), modes), dma((len(GATHER),)), dma((modes + 1,)),
             *two(SLICES, cores), *two(SLICES, modes), *two(SLICES, depth), *two(SLICES, depth),
@@ -499,8 +565,31 @@
     )(unfolded, start_block)
 
 
+def emit_kernel(*refs):
+    count = len(refs) // 2
+    sem = refs[-1]
+    copies = [pltpu.make_async_copy(refs[k], refs[count + k], sem.at[k]) for k in range(count)]
+    for copy in copies:
+        copy.start()
+    for copy in copies:
+        copy.wait()
+
+
+def emit(*arrays):
+    count = len(arrays)
+    return pl.pallas_call(
+        emit_kernel,
+        out_shape=tuple(jax.ShapeDtypeStruct(x.shape, x.dtype) for x in arrays),
+        in_specs=[pl.BlockSpec(memory_space=pl.ANY)] * count,
+        out_specs=(pl.BlockSpec(memory_space=pltpu.HBM),) * count,
+        scratch_shapes=[pltpu.SemaphoreType.DMA((count,))],
+        compiler_params=pltpu.CompilerParams(vmem_limit_bytes=1024 * 1024),
+        name="emit",
+    )(*arrays)
+
+
 def per_device(unfolded, start_block):
-    return program(unfolded, start_block, lax.axis_size("mode"), lax.axis_size("rest"))
+    return emit(*program(unfolded, start_block, lax.axis_size("mode"), lax.axis_size("rest")))
 
 
 def solution(mesh):

time: 106 us -> 99.4 us (0.938)
  Pallas kernels: 101 us -> 96.9 us
  local copies, waits for them, and re-layouts: 3.59 us -> 0.94 us
    pallas_call x1, Pallas kernels: 101 us -> 95.5 us  [program(): pl.pallas_call(functools.partial(kernel, (modes, cores, depth), cols_dev...]
    unnamed x5 -> x2, local copies, waits for them, and re-layouts: 3.59 us -> 0.94 us
    pallas_call x0 -> x1, Pallas kernels: none -> 1.43 us  [emit(): pl.pallas_call(emit_kernel, out_shape=tuple((jax.ShapeDtypeStruct(x.shape...]
where the time goes in v2:
time: 99.4 us; the launch traced here: 98.6 us
  Pallas kernels  96.9 us (97%)
    pallas_call x1, Pallas kernels, program(): pl.pallas_call(functools.partial(kernel, (modes, cores, depth), cols_dev...  95.5 us

profile of v2, /device:TPU:0, one launch (start us, length us, event | category | flops | bytes accessed | tf_op | source)
XLA Modules:
  0.0 98.6 jit_solution(9410557120862519831)
XLA Ops:
  0.6 0.0 copy-start
  0.6 0.9 copy-done
  1.6 95.5 %truncate.1 = (f32[512,512]{1,0:T(8,128)S(1)}, f32[512,128]{1,0:T(8,128)S(1)}, f32[32,8192]{1,0:T(8,128)S(1)}) custom-call(f32[128,8192]{1,0:T(8,128)} %x_ref.1, f32[512,128]{1,0:T(8,128)S(1)} %copy-done), custom_call_target="tpu_custom_call" | custom-call | tf_op jit(solution)/shard_map/truncate/pallas_call | solution.py:523
  97.0 1.4 %emit.1 = (f32[512,512]{1,0:T(8,128)}, f32[512,128]{1,0:T(8,128)}, f32[32,8192]{1,0:T(8,128)}) custom-call(f32[512,512]{1,0:T(8,128)S(1)} %get-tuple-element.6.refs_0_, f32[512,128]{1,0:T(8,128)S(1)} %get-tuple-element.7.refs_1_, f32[32,8192]{1,0:T(8,128)S(1)} %get-tuple-element.8.refs_2_), custom_call_target="tpu_custom_call" | custom-call | tf_op jit(solution)/shard_map/emit/pallas_call | solution.py:580
Async XLA Ops:
  0.6 1.0 copy-start

commit v3 on v2

--- a/solution.py
+++ b/solution.py
@@ -151,13 +151,13 @@
     return (depth // 4, depth // 2) if depth % 4 == 0 else (0, depth)
 
 
-GATHER = (3, 2, 2, 1)
+GATHER = (6, 4, 3, 2, 1)
 SCATTER = (1, 1, 2, 2, 2)
 
 
 def kernel(shape, total_cols, x_ref, start_ref, tri_ref, factor_ref, core_ref,
            full, hi_ref, lo_ref, own, part, acc, tot, dacc, dtot, got_c, got_m, got_z, sum1, sum2, dgot_c, dgot_z,
-           work, gram_h, gram_m, gram_l, small, panel, basis, begin,
+           work, gram_h, gram_m, gram_l, small, panel, basis, pieces_ref, begin,
            row_s, row_r, row_l, own_l, c_s, c_r, m_s, m_r, z_s, z_r, az_s, az_r, am_s, am_r, ac_s, ac_r,
            dc_s, dc_r, dz_s, dz_r, dm_s, dm_r, df_s, df_r, out_s, out_r):
     modes, cores, depth = shape
@@ -248,6 +248,23 @@
 
     pairs = off_pairs(rounds)
 
+    padded = acc.shape[0]
+    h0 = padded // SLICES
+    h1 = h0 // cores
+    h2 = h1 // modes
+    h3 = h2 // owners
+    sends = []
+    stage_c = []
+
+    def begin_slice(s):
+        batch = []
+        for off in range(1, cores):
+            other, device = core_peer(off)
+            copy = remote(acc.at[at(s * h0 + other * h1, h1)], got_c.at[s, off - 1], c_s.at[s, off], c_r.at[s, off], device)
+            copy.start()
+            batch.append(copy)
+        stage_c.append(batch)
+
     def absorb(c):
         for copy in arrivals[c]:
             copy.wait()
@@ -263,9 +280,14 @@
             for j in range(i + 1, rounds):
                 spot = pl.ds(pairs.index((i, j)) * LANES, LANES)
                 acc[spot, :] += strip[:, (j - i - 1) * LANES : (j - i) * LANES]
+            if c == len(pieces) - 1:
+                done = len([p for p in pairs if p[0] <= i]) * LANES
+                while (len(stage_c) + 1) * h0 <= done:
+                    begin_slice(len(stage_c))
 
     absorb(0)
     fetch.wait()
+    pieces_ref[...] = stack(parts3(begin[...].T))
     for copy in pending:
         copy.wait()
     value = dacc[at(me_core * half, half), :]
@@ -286,22 +308,8 @@
     for c in range(2, len(pieces)):
         absorb(c)
 
-    padded = acc.shape[0]
-    h0 = padded // SLICES
-    h1 = h0 // cores
-    h2 = h1 // modes
-    h3 = h2 // owners
-    sends = []
-
-    stage_c = []
-    for s in range(SLICES):
-        batch = []
-        for off in range(1, cores):
-            other, device = core_peer(off)
-            copy = remote(acc.at[at(s * h0 + other * h1, h1)], got_c.at[s, off - 1], c_s.at[s, off], c_r.at[s, off], device)
-            copy.start()
-            batch.append(copy)
-        stage_c.append(batch)
+    for s in range(len(stage_c), SLICES):
+        begin_slice(s)
     stage_m = []
     for s in range(SLICES):
         value = acc[at(s * h0 + me_core * h1, h1), :]
@@ -324,7 +332,7 @@
         copy.start()
         stage_d.append(copy)
 
-    def forward(ref, spot, send, recv):
+    def forward(relays, ref, spot, send, recv):
         for off in range(1, cores):
             _, device = core_peer(off)
             copy = remote(ref.at[spot], ref.at[spot], send.at[off], recv.at[off], device)
@@ -338,7 +346,7 @@
         for ref, value in zip((gram_h, gram_m, gram_l), parts3(piece)):
             ref[spot] = value.astype(BF16)
 
-    forward(dtot, dmine, df_s.at[0], df_r.at[0])
+    forward(relays, dtot, dmine, df_s.at[0], df_r.at[0])
 
     def z_copy(s, off):
         other, device = z_peer(off)
@@ -382,11 +390,10 @@
     for off, copy in enumerate(stage_d, 1):
         copy.wait_recv()
         source = lax.rem(me_mode - off + modes, modes)
-        forward(dtot, at(source * rows_dev + me_core * half, half), df_s.at[off], df_r.at[off])
+        forward(relays, dtot, at(source * rows_dev + me_core * half, half), df_s.at[off], df_r.at[off])
     sends += stage_d
     for copy in relays:
         copy.wait_recv()
-    relays.clear()
     for i in range(rounds):
         spot = (pl.ds(i * LANES, LANES), pl.ds(i * LANES, LANES))
         piece = dtot[pl.ds(i * LANES, LANES), :]
@@ -396,6 +403,7 @@
     invert(panel, 0)
 
     stage_a = []
+    hops = []
     for s in range(SLICES):
         def arrive(off):
             source = lax.rem(me_z - off + depth, depth)
@@ -408,29 +416,30 @@
             copy = remote(tot.at[block], tot.at[block], am_s.at[s, off], am_r.at[s, off], device)
             copy.start()
             batch.append(copy)
-        forward(tot, block, ac_s.at[s, 0], ac_r.at[s, 0])
+        hops.append([])
+        forward(hops[s], tot, block, ac_s.at[s, 0], ac_r.at[s, 0])
         stage_a.append(batch)
     for s in range(SLICES):
         for off, copy in enumerate(stage_a[s], 1):
             copy.wait_recv()
             source = lax.rem(me_mode - off + modes, modes)
-            forward(tot, at(s * h0 + me_core * h1 + source * h2, h2), ac_s.at[s, off], ac_r.at[s, off])
+            forward(hops[s], tot, at(s * h0 + me_core * h1 + source * h2, h2), ac_s.at[s, off], ac_r.at[s, off])
         sends += stage_a[s]
-    for copy in relays:
-        copy.wait_recv()
-
-    for where, (i, j) in enumerate(pairs):
-        piece = tot[pl.ds(where * LANES, LANES), :]
-        spot = (pl.ds(i * LANES, LANES), pl.ds(j * LANES, LANES))
-        work[spot] = piece
-        keep_gram(spot, piece)
-        keep_gram(spot[::-1], piece.T)
-
-    basis[...] = begin[...].T
+    for s in range(SLICES):
+        for copy in hops[s]:
+            copy.wait_recv()
+        for where, (i, j) in enumerate(pairs):
+            if (where * LANES + LANES - 1) // h0 == s:
+                piece = tot[pl.ds(where * LANES, LANES), :]
+                spot = (pl.ds(i * LANES, LANES), pl.ds(j * LANES, LANES))
+                work[spot] = piece
+                keep_gram(spot, piece)
+                keep_gram(spot[::-1], piece.T)
+
     r = basis.shape[0]
 
     def iterate(t, carry):
-        old = stack(parts3(basis[...]))
+        old = pieces_ref[...]
         one = nn(old, gram_h[...])
         two = nn(old[: 2 * r], gram_m[...])
         image = one[:r] + ((one[r : 2 * r] + two[:r]) + (one[2 * r :] + (two[r:] + nn(old[:r], gram_l[...]))))
@@ -443,12 +452,14 @@
         wh, wm, wl = parts3(lower_part(small[...]))
         high = nn(stack([stack([wh, wh], 1), stack([wm, wm], 1)]), new[: 2 * r])
         rest = nn(stack([wl, wh], 1), stack([ih, il]))
-        basis[...] = high[:r] + (high[r:] + rest)
+        result = high[:r] + (high[r:] + rest)
+        basis[...] = result
+        pieces_ref[...] = stack(parts3(result))
         return carry
 
     lax.fori_loop(0, ITERS, iterate, 0)
     basis_t = basis[...]
-    bh, bl = split(basis_t)
+    bh, bl = pieces_ref[:r, :], pieces_ref[r : 2 * r, :]
     out_rows = core_ref.shape[0]
     for c, (start, size) in enumerate(cuts(width, SCATTER)):
         cols = pl.ds(start, size)
@@ -551,6 +562,7 @@
             pltpu.VMEM((r, r), F32),
             pltpu.VMEM((m, LANES), F32),
             pltpu.VMEM((r, m), F32),
+            pltpu.VMEM((3 * r, m), BF16),
             pltpu.VMEM((m, r), F32),
             *two(len(GATHER), modes), dma((len(GATHER),)), dma((modes + 1,)),
             *two(SLICES, cores), *two(SLICES, modes), *two(SLICES, depth), *two(SLICES, depth),
@@ -562,7 +574,7 @@
             collective_id=0, has_side_effects=True, vmem_limit_bytes=48 * 1024 * 1024
         ),
         name="truncate",
-    )(unfolded, start_block)
+    )(unfolded, pltpu.with_memory_space_constraint(start_block, pltpu.HBM))
 
 
 def emit_kernel(*refs):

time: 99.4 us -> 98.4 us (0.990)
  no operation moved by 1% of the time
where the time goes in v3:
time: 98.4 us; the launch traced here: 98.1 us
  Pallas kernels  97.3 us (99%)
    pallas_call x1, Pallas kernels, program(): pl.pallas_call(functools.partial(kernel, (modes, cores, depth), cols_dev...  95.9 us

profile of v3, /device:TPU:0, one launch (start us, length us, event | category | flops | bytes accessed | tf_op | source)
XLA Modules:
  0.0 98.1 jit_solution(13614479693693386263)
XLA Ops:
  0.6 95.9 %truncate.1 = (f32[512,512]{1,0:T(8,128)S(1)}, f32[512,128]{1,0:T(8,128)S(1)}, f32[32,8192]{1,0:T(8,128)S(1)}) custom-call(f32[128,8192]{1,0:T(8,128)} %x_ref.1, f32[512,128]{1,0:T(8,128)} %start_ref.1), custom_call_target="tpu_custom_call" | custom-call | tf_op jit(solution)/shard_map/truncate/pallas_call | solution.py:534
  96.5 1.4 %emit.1 = (f32[512,512]{1,0:T(8,128)}, f32[512,128]{1,0:T(8,128)}, f32[32,8192]{1,0:T(8,128)}) custom-call(f32[512,512]{1,0:T(8,128)S(1)} %get-tuple-element.6.refs_0_, f32[512,128]{1,0:T(8,128)S(1)} %get-tuple-element.7.refs_1_, f32[32,8192]{1,0:T(8,128)S(1)} %get-tuple-element.8.refs_2_), custom_call_target="tpu_custom_call" | custom-call | tf_op jit(solution)/shard_map/emit/pallas_call | solution.py:592

commit v4 on v3

--- a/solution.py
+++ b/solution.py
@@ -68,9 +68,6 @@
     for first in range(0, MACRO, MICRO):
         stop = first + MICRO
         cols = {(j, h): column(rows[h], r0 + j) for j in range(first, stop) for h in range(j // SUB, tiles)}
-        unit = spread(cols[first, first // SUB], first % SUB)
-        scale = 1.0 / unit
-        cols = {spot: x * scale for spot, x in cols.items()}
         for k in range(first, stop, 2):
             t, s = divmod(k, SUB)
             p = spread(cols[k, t], s)
@@ -79,7 +76,7 @@
             det = p * b - a * a
             inv_p = 1.0 / p
             inv_q = p * (1.0 / det)
-            found = jnp.where(sub == s, p, det * inv_p) * unit
+            found = jnp.where(sub == s, p, det * inv_p)
             pivots[t] = found if s == 0 else jnp.where(sub >= s, found, pivots[t])
             f = {h: cols[k, h] * inv_p for h in range(t, tiles)}
             f[t] = jnp.where(sub > s, f[t], 0.0)
@@ -126,6 +123,20 @@
     return jnp.concatenate(pieces, axis=axis).astype(BF16)
 
 
+def invert_scaled(ref, base):
+    spot = pl.ds(base, LANES)
+    block = ref[spot, :]
+    row = lax.broadcasted_iota(jnp.int32, block.shape, 0)
+    col = lax.broadcasted_iota(jnp.int32, block.shape, 1)
+    diagonal = jnp.where(row == col, block, 0.0)
+    below = lax.rsqrt(jnp.sum(diagonal, axis=1, keepdims=True))
+    size = jnp.sum(diagonal, axis=0, keepdims=True)
+    across = lax.rsqrt(size)
+    ref[spot, :] = (block * below) * across
+    invert(ref, base)
+    ref[spot, :] = ref[spot, :] * jnp.where(row >= col, across, size * across)
+
+
 def lower_part(x):
     row = lax.broadcasted_iota(jnp.int32, x.shape, 0)
     col = lax.broadcasted_iota(jnp.int32, x.shape, 1)
@@ -400,7 +411,7 @@
         keep_gram(spot, piece)
         work[spot] = piece
     panel[pl.ds(0, LANES), :] = dtot[pl.ds(0, LANES), :]
-    invert(panel, 0)
+    invert_scaled(panel, 0)
 
     stage_a = []
     hops = []
@@ -443,6 +454,7 @@
         one = nn(old, gram_h[...])
         two = nn(old[: 2 * r], gram_m[...])
         image = one[:r] + ((one[r : 2 * r] + two[:r]) + (one[2 * r :] + (two[r:] + nn(old[:r], gram_l[...]))))
+        image = image * lax.rsqrt(jnp.sum(image * image, axis=1, keepdims=True))
         ih, im, il = parts3(image)
         new = stack([ih, im, il])
         q = nt(new, new[: 2 * r])
@@ -482,7 +494,7 @@
         here = pl.ds(base, LANES)
         if t > 0:
             panel[here, :] = work[here, here]
-            invert(panel, base)
+            invert_scaled(panel, base)
         if t < rounds - 1:
             tail = pl.ds(base + LANES, m - base - LANES)
             u = dotf(lower_part(panel[here, :]), work[here, tail], ((1,), (0,)))

time: 98.4 us -> 98.9 us (level)
  no operation moved by 1% of the time
where the time goes in v4:
time: 98.9 us; the launch traced here: 98.5 us
  Pallas kernels  97.7 us (99%)
    pallas_call x1, Pallas kernels, program(): pl.pallas_call(functools.partial(kernel, (modes, cores, depth), cols_dev...  96.2 us

profile of v4, /device:TPU:0, one launch (start us, length us, event | category | flops | bytes accessed | tf_op | source)
XLA Modules:
  0.0 98.5 jit_solution(13623342069869592740)
XLA Ops:
  0.6 96.2 %truncate.1 = (f32[512,512]{1,0:T(8,128)S(1)}, f32[512,128]{1,0:T(8,128)S(1)}, f32[32,8192]{1,0:T(8,128)S(1)}) custom-call(f32[128,8192]{1,0:T(8,128)} %x_ref.1, f32[512,128]{1,0:T(8,128)} %start_ref.1), custom_call_target="tpu_custom_call" | custom-call | tf_op jit(solution)/shard_map/truncate/pallas_call | solution.py:546
  96.9 1.4 %emit.1 = (f32[512,512]{1,0:T(8,128)}, f32[512,128]{1,0:T(8,128)}, f32[32,8192]{1,0:T(8,128)}) custom-call(f32[512,512]{1,0:T(8,128)S(1)} %get-tuple-element.6.refs_0_, f32[512,128]{1,0:T(8,128)S(1)} %get-tuple-element.7.refs_1_, f32[32,8192]{1,0:T(8,128)S(1)} %get-tuple-element.8.refs_2_), custom_call_target="tpu_custom_call" | custom-call | tf_op jit(solution)/shard_map/emit/pallas_call | solution.py:604

commit v5 on v4

--- a/solution.py
+++ b/solution.py
@@ -454,14 +454,18 @@
         one = nn(old, gram_h[...])
         two = nn(old[: 2 * r], gram_m[...])
         image = one[:r] + ((one[r : 2 * r] + two[:r]) + (one[2 * r :] + (two[r:] + nn(old[:r], gram_l[...]))))
-        image = image * lax.rsqrt(jnp.sum(image * image, axis=1, keepdims=True))
+        below = lax.rsqrt(jnp.sum(image * image, axis=1, keepdims=True))
         ih, im, il = parts3(image)
         new = stack([ih, im, il])
         q = nt(new, new[: 2 * r])
         low = q[2 * r :, :r]
-        small[...] = q[:r, :r] + ((q[:r, r:] + q[r : 2 * r, :r]) + (q[r : 2 * r, r:] + (low + low.T)))
+        gram = q[:r, :r] + ((q[:r, r:] + q[r : 2 * r, :r]) + (q[r : 2 * r, r:] + (low + low.T)))
+        row = lax.broadcasted_iota(jnp.int32, (r, r), 0)
+        col = lax.broadcasted_iota(jnp.int32, (r, r), 1)
+        across = lax.rsqrt(jnp.sum(jnp.where(row == col, gram, 0.0), axis=0, keepdims=True))
+        small[...] = (gram * below) * across
         invert(small, 0)
-        wh, wm, wl = parts3(lower_part(small[...]))
+        wh, wm, wl = parts3(lower_part(small[...]) * across)
         high = nn(stack([stack([wh, wh], 1), stack([wm, wm], 1)]), new[: 2 * r])
         rest = nn(stack([wl, wh], 1), stack([ih, il]))
         result = high[:r] + (high[r:] + rest)

time: 98.9 us -> 98.8 us (level)
  no operation moved by 1% of the time
where the time goes in v5:
time: 98.8 us; the launch traced here: 98.4 us
  Pallas kernels  97.6 us (99%)
    pallas_call x1, Pallas kernels, program(): pl.pallas_call(functools.partial(kernel, (modes, cores, depth), cols_dev...  96.2 us

profile of v5, /device:TPU:0, one launch (start us, length us, event | category | flops | bytes accessed | tf_op | source)
XLA Modules:
  0.0 98.4 jit_solution(11253302158578550092)
XLA Ops:
  0.6 96.2 %truncate.1 = (f32[512,512]{1,0:T(8,128)S(1)}, f32[512,128]{1,0:T(8,128)S(1)}, f32[32,8192]{1,0:T(8,128)S(1)}) custom-call(f32[128,8192]{1,0:T(8,128)} %x_ref.1, f32[512,128]{1,0:T(8,128)} %start_ref.1), custom_call_target="tpu_custom_call" | custom-call | tf_op jit(solution)/shard_map/truncate/pallas_call | solution.py:550
  96.8 1.4 %emit.1 = (f32[512,512]{1,0:T(8,128)}, f32[512,128]{1,0:T(8,128)}, f32[32,8192]{1,0:T(8,128)}) custom-call(f32[512,512]{1,0:T(8,128)S(1)} %get-tuple-element.6.refs_0_, f32[512,128]{1,0:T(8,128)S(1)} %get-tuple-element.7.refs_1_, f32[32,8192]{1,0:T(8,128)S(1)} %get-tuple-element.8.refs_2_), custom_call_target="tpu_custom_call" | custom-call | tf_op jit(solution)/shard_map/emit/pallas_call | solution.py:608
